TPU v7x, 32 devices: a whole 2x2x4 slice. The times are simulated.
32 devices in a mesh: space: 8 (over z, x), filt: 4 (over y, core).
Axes of the slice: x: 2, y: 2, z: 4, core: 2. Of those that a mesh axis runs over, the one named last changes fastest.
Arguments:
- inputs: bfloat16 [16, 4, 32, 512], P('space'), may hold values from -6 to 6
- pre_hidden: bfloat16 [16, 4, 32, 512], P('space'), may hold values from -6 to 6
- weight_one: bfloat16 [512, 3, 3, 3, 512], P(None, None, None, None, 'filt'), may hold values from -0.0546875 to 0.0546875
- weight_two: bfloat16 [512, 3, 3, 3, 512], P(None, None, None, None, 'filt'), may hold values from -0.0546875 to 0.0546875
- grad_out: bfloat16 [16, 4, 32, 512], P('space', None, None, 'filt'), may hold values from -6 to 6
Outputs:
- grad_inputs: bfloat16 [16, 4, 32, 512], P('space', 'filt')
- grad_one: float32 [512, 3, 3, 3, 512], P('space', None, None, None, 'filt')
- grad_two: float32 [512, 3, 3, 3, 512], P('space', None, None, None, 'filt')
All inputs are finite; a program needn't handle non-finite values.
Results may differ from a plain program's by a relative error of at most 0.0049.
Values may be sent and summed in bfloat16 or wider, within the bound.
A program may use at most 128 MiB of HBM per device.

v0:
```python
import math
import jax
import jax.numpy as jnp
from jax import lax
from jax.sharding import PartitionSpec as P

TAP_LIST = [
    (tap_depth, tap_row, tap_col)
    for tap_depth in range(3)
    for tap_row in range(3)
    for tap_col in range(3)
]


def window_at(padded, tap, planes, height, columns):
    return padded[
        2 - tap[0] : 2 - tap[0] + planes,
        2 - tap[1] : 2 - tap[1] + height,
        2 - tap[2] : 2 - tap[2] + columns,
        :,
    ]


def carry_back(padded, weight, planes, height, columns):
    channels = weight.shape[4]
    summed = jnp.zeros((planes * height * columns, weight.shape[0]), jnp.float32)
    for tap in TAP_LIST:
        window = window_at(padded, tap, planes, height, columns).reshape(-1, channels)
        summed = summed + lax.dot_general(
            window,
            weight[:, tap[0], tap[1], tap[2], :],
            (((1,), (1,)), ((), ())),
            preferred_element_type=jnp.float32,
        )
    return summed.reshape(planes, height, columns, weight.shape[0])


def weight_terms(source, padded, planes, height, columns, factor):
    channels = padded.shape[3]
    pieces = []
    for tap in TAP_LIST:
        window = window_at(padded, tap, planes, height, columns).reshape(-1, channels)
        pieces.append(
            lax.dot_general(
                source, window, (((1,), (0,)), ((), ())), preferred_element_type=jnp.float32
            )
            * factor
        )
    return jnp.stack(pieces, axis=1).reshape(source.shape[0], 3, 3, 3, channels)


def pad_all(field):
    return jnp.pad(field, ((1, 1), (1, 1), (1, 1), (0, 0)))


def shards(inputs, pre_hidden, weight_one, weight_two, grad_out):
    planes, height, columns, in_channels = inputs.shape
    mid_channels = pre_hidden.shape[3]
    count = lax.axis_size("space")
    voxel_local = planes * height * columns
    factor = 1.0 / math.sqrt(voxel_local * count)
    start = lax.axis_index("space") * planes
    out_all = pad_all(lax.all_gather(grad_out, "space", axis=0, tiled=True))
    out_pad = lax.dynamic_slice_in_dim(out_all, start, planes + 2, 0)
    activity = jnp.maximum(pre_hidden, jnp.zeros_like(pre_hidden))
    both = jnp.stack([activity, inputs]).reshape(2, voxel_local, in_channels)
    both = jnp.swapaxes(both, 1, 2).reshape(2, count, in_channels // count, voxel_local)
    both = lax.all_to_all(both, "space", 1, 1)
    both = jnp.swapaxes(both, 1, 2).reshape(2, in_channels // count, count * voxel_local)
    hidden_partial = carry_back(out_pad, weight_two, planes, height, columns)
    grad_hidden = lax.psum_scatter(hidden_partial, "filt", scatter_dimension=3, tiled=True)
    group_width = grad_hidden.shape[3]
    own_pre = lax.dynamic_slice_in_dim(
        pre_hidden, lax.axis_index("filt") * group_width, group_width, 3
    )
    grad_pre = jnp.where(own_pre > 0, grad_hidden, jnp.zeros_like(grad_hidden)).astype(jnp.bfloat16)
    pre_all = pad_all(lax.all_gather(grad_pre, "space", axis=0, tiled=True))
    pre_pad = lax.dynamic_slice_in_dim(pre_all, start, planes + 2, 0)
    input_partial = carry_back(pre_pad, weight_one, planes, height, columns)
    grad_rows = lax.psum_scatter(input_partial, "filt", scatter_dimension=1, tiled=True)
    grad_inputs = grad_rows.astype(jnp.bfloat16)
    depth = planes * count
    grad_two = weight_terms(both[0], out_all, depth, height, columns, factor)
    grad_one = weight_terms(both[1], pre_all, depth, height, columns, factor)
    return (grad_inputs, grad_one, grad_two)


def solution(mesh):
    placed = (
        P("space", None, None, None),
        P("space", None, None, None),
        P(None, None, None, None, "filt"),
        P(None, None, None, None, "filt"),
        P("space", None, None, "filt"),
    )
    return jax.shard_map(
        shards,
        mesh=mesh,
        in_specs=placed,
        out_specs=(
            P("space", "filt", None, None),
            P("space", None, None, None, "filt"),
            P("space", None, None, None, "filt"),
        ),
        check_vma=False,
    )
```

profile of v0, /device:TPU:0, one launch (start us, length us, event | category | flops | bytes accessed | tf_op | source)
XLA Modules:
  0.0 189.9 jit_solution(2208045454308915686)
XLA Ops:
  10.2 7.3 %all-to-all-start = ((bf16[2,8,64,256]{3,2,0,1:T(8,128)(2,1)}), bf16[2,8,64,256]{3,2,0,1:T(8,128)(2,1)}, u32[]{:S(2)}, u32[]{:S(2)}) async-start(bf16[2,8,64,256]{3,2,0,1:T(8,128)(2,1)} %copy.16), calls=%async_computation.1 | async-start | bytes 1048576 | tf_op jit(solution)/shard_map/all_to_all | solution.py:68
  17.6 38.5 %all_gather.6 = bf16[16,4,32,128]{3,2,1,0:T(8,128)(2,1)S(1)} all-gather(bf16[2,4,32,128]{3,2,1,0:T(8,128)(2,1)S(1)} %copy-done.36), channel_id=1, replica_groups=mesh['space'=8,'filt'=4] {'space'}, dimensions={0}, use_global_device_ids=true | all-gather | bytes 589824 | tf_op jit(solution)/shard_map/all_gather | solution.py:63
  57.9 1.1 fusion.162
  59.0 1.1 convolution_add_fusion.51
  60.1 1.1 convolution_add_fusion.50
  61.3 1.1 convolution_add_fusion.49
  67.6 1.0 convolution_add_fusion.26
  69.3 2.2 %pad_slice_fusion.27 = (bf16[16,4,32,128]{3,2,1,0:T(8,128)(2,1)}, bf16[16,4,32,128]{3,2,1,0:T(8,128)(2,1)}, bf16[16,4,32,128]{3,2,1,0:T(8,128)(2,1)}, bf16[16,4,...) fusion(bf16[16,4,32,128]{3,2,1,0:T(8,128)(2,1)S(1)} %all_gather.6), kind=kLoop, calls=%fused_computation.80 | loop fusion | bytes 4194304 | tf_op jit(solution)/shard_map/slice | solution.py:16
  71.5 4.4 %pad_slice_fusion.26 = (bf16[16,4,32,128]{3,2,1,0:T(8,128)(2,1)S(1)}, bf16[16,4,32,128]{3,2,1,0:T(8,128)(2,1)}, bf16[16,4,32,128]{3,2,1,0:T(8,128)(2,1)}, bf16[1...) fusion(bf16[16,4,32,128]{3,2,1,0:T(8,128)(2,1)S(1)} %all_gather.6), kind=kLoop, calls=%fused_computation.79 | loop fusion | bytes 10485760 | tf_op jit(solution)/shard_map/slice | solution.py:16
  75.9 1.2 fusion.218
  77.2 2.0 %fusion.53 = f32[64,27,128]{2,0,1:T(8,128)} fusion(bf16[64,2048]{1,0:T(8,128)(2,1)S(1)} %bitcast.700, bf16[2048,128]{1,0:T(8,128)(2,1)} %bitcast.766), kind=kOutput, calls=%fused_computation.238 | convolution fusion | flops 33562624 | bytes 819200 | tf_op jit(solution)/shard_map/dot_general | solution.py:44
  79.2 1.9 %fusion.51 = f32[64,27,128]{2,0,1:T(8,128)} fusion(f32[64,27,128]{2,0,1:T(8,128)} %fusion.53, bf16[64,2048]{1,0:T(8,128)(2,1)S(1)} %bitcast.701, bf16[2048,128]{1,0:T(8,128)(2,1)} %bitcast.765), kind=kOutput, calls=%fused_computation.235 | convolution fusion | flops 33562624 | bytes 819200 | tf_op jit(solution)/shard_map/dot_general | solution.py:44
  81.1 2.0 %fusion.49 = f32[64,27,128]{2,0,1:T(8,128)} fusion(f32[64,27,128]{2,0,1:T(8,128)} %fusion.51, bf16[64,2048]{1,0:T(8,128)(2,1)S(1)} %bitcast.702, bf16[2048,128]{1,0:T(8,128)(2,1)} %bitcast.764), kind=kOutput, calls=%fused_computation.232 | convolution fusion | flops 33562624 | bytes 819200 | tf_op jit(solution)/shard_map/dot_general | solution.py:44
  104.4 31.5 %all_gather.7 = bf16[16,4,32,128]{3,2,1,0:T(8,128)(2,1)S(1)} all-gather(bf16[2,4,32,128]{3,2,1,0:T(8,128)(2,1)S(1)} %select_convert_fusion), channel_id=1, replica_groups=mesh['space'=8,'filt'=4] {'space'}, dimensions={0}, use_global_device_ids=true | all-gather | bytes 589824 | tf_op jit(solution)/shard_map/all_gather | solution.py:77
  135.8 4.5 %pad_slice_fusion = (bf16[16,4,32,128]{3,2,1,0:T(8,128)(2,1)S(1)}, bf16[16,4,32,128]{3,2,1,0:T(8,128)(2,1)}, bf16[16,4,32,128]{3,2,1,0:T(8,128)(2,1)}, bf16[16,4...) fusion(bf16[16,4,32,128]{3,2,1,0:T(8,128)(2,1)S(1)} %all_gather.7), kind=kLoop, calls=%fused_computation.26 | loop fusion | bytes 10485760 | tf_op jit(solution)/shard_map/slice | solution.py:16
  140.3 2.2 %pad_slice_fusion.1 = (bf16[16,4,32,128]{3,2,1,0:T(8,128)(2,1)}, bf16[16,4,32,128]{3,2,1,0:T(8,128)(2,1)}, bf16[16,4,32,128]{3,2,1,0:T(8,128)(2,1)}, bf16[16,4,3...) fusion(bf16[16,4,32,128]{3,2,1,0:T(8,128)(2,1)S(1)} %all_gather.7), kind=kLoop, calls=%fused_computation.27 | loop fusion | bytes 4194304 | tf_op jit(solution)/shard_map/slice | solution.py:16
  150.4 1.0 convolution_add_fusion
  151.4 17.4 %all-reduce.4 = bf16[2,4,32,512]{3,2,1,0:T(8,128)(2,1)} all-reduce(f32[2,4,32,512]{3,2,1,0:T(8,128)} %bitcast.768), channel_id=3, replica_groups=mesh['space'=8,'filt'=4] {'filt'}, use_global_device_ids=true, to_apply=%region_1.2.clone | all-reduce | flops 131072 | bytes 786432
  168.8 1.4 fusion.107
  170.3 1.3 fusion.105
  171.6 1.3 fusion.103
  172.9 1.3 fusion.101
  174.3 1.3 fusion.99
  180.9 2.1 %dynamic-slice_convert_fusion = bf16[2,1,32,512]{3,2,1,0:T(8,128)(2,1)} fusion(bf16[2,4,32,512]{3,2,1,0:T(8,128)(2,1)} %all-reduce.4, u32[]{:T(128)} %bitcast.231), kind=kLoop, calls=%fused_computation.321 | loop fusion | bytes 131076 | tf_op jit(solution)/shard_map/convert_element_type | solution.py:81
  (188 shorter events, 44.5 us)
Async XLA Ops:
  7.2 10.4 %copy-start.36 = (bf16[2,4,32,128]{3,2,1,0:T(8,128)(2,1)S(1)}, bf16[2,4,32,128]{3,2,1,0:T(8,128)(2,1)}, u32[]{:S(2)}) copy-start(bf16[2,4,32,128]{3,2,1,0:T(8,128)(2,1)} %param.9) | copy-start | bytes 196612
  10.2 65.7 %all-to-all-start = ((bf16[2,8,64,256]{3,2,0,1:T(8,128)(2,1)}), bf16[2,8,64,256]{3,2,0,1:T(8,128)(2,1)}, u32[]{:S(2)}, u32[]{:S(2)}) async-start(bf16[2,8,64,256]{3,2,0,1:T(8,128)(2,1)} %copy.16), calls=%async_computation.1 | async-start | bytes 1048576 | tf_op jit(solution)/shard_map/all_to_all | solution.py:68
  17.5 85.9 %reduce-scatter.5.cloned.1.call-start = ((), (), s32[]{:S(2)}) async-start(), calls=%async_computation.2 | async-start | bytes 655360 | tf_op jit(solution)/shard_map/reduce_scatter | solution.py:71
  75.9 7.2 %copy-start.21 = (bf16[16,4,32,128]{3,2,1,0:T(8,128)(2,1)S(1)}, bf16[16,4,32,128]{3,2,1,0:T(8,128)(2,1)}, u32[]{:S(2)}) copy-start(bf16[16,4,32,128]{3,2,1,0:T(8,128)(2,1)} %get-tuple-element.7) | copy-start | bytes 1572868
  75.9 8.1 %copy-start.20 = (bf16[16,4,32,128]{3,2,1,0:T(8,128)(2,1)S(1)}, bf16[16,4,32,128]{3,2,1,0:T(8,128)(2,1)}, u32[]{:S(2)}) copy-start(bf16[16,4,32,128]{3,2,1,0:T(8,128)(2,1)} %get-tuple-element.8) | copy-start | bytes 1572868
  75.9 8.9 %copy-start.19 = (bf16[16,4,32,128]{3,2,1,0:T(8,128)(2,1)S(1)}, bf16[16,4,32,128]{3,2,1,0:T(8,128)(2,1)}, u32[]{:S(2)}) copy-start(bf16[16,4,32,128]{3,2,1,0:T(8,128)(2,1)} %get-tuple-element.9) | copy-start | bytes 1572868
  75.9 9.7 %copy-start.18 = (bf16[16,4,32,128]{3,2,1,0:T(8,128)(2,1)S(1)}, bf16[16,4,32,128]{3,2,1,0:T(8,128)(2,1)}, u32[]{:S(2)}) copy-start(bf16[16,4,32,128]{3,2,1,0:T(8,128)(2,1)} %get-tuple-element.10) | copy-start | bytes 1572868
  75.9 10.6 %copy-start.17 = (bf16[16,4,32,128]{3,2,1,0:T(8,128)(2,1)S(1)}, bf16[16,4,32,128]{3,2,1,0:T(8,128)(2,1)}, u32[]{:S(2)}) copy-start(bf16[16,4,32,128]{3,2,1,0:T(8,128)(2,1)} %get-tuple-element.11) | copy-start | bytes 1572868
  77.2 10.2 %copy-start.16 = (bf16[16,4,32,128]{3,2,1,0:T(8,128)(2,1)S(1)}, bf16[16,4,32,128]{3,2,1,0:T(8,128)(2,1)}, u32[]{:S(2)}) copy-start(bf16[16,4,32,128]{3,2,1,0:T(8,128)(2,1)} %get-tuple-element.12) | copy-start | bytes 1572868
  77.2 11.0 %copy-start.15 = (bf16[16,4,32,128]{3,2,1,0:T(8,128)(2,1)S(1)}, bf16[16,4,32,128]{3,2,1,0:T(8,128)(2,1)}, u32[]{:S(2)}) copy-start(bf16[16,4,32,128]{3,2,1,0:T(8,128)(2,1)} %get-tuple-element.13) | copy-start | bytes 1572868
  79.2 9.9 %copy-start.14 = (bf16[16,4,32,128]{3,2,1,0:T(8,128)(2,1)S(1)}, bf16[16,4,32,128]{3,2,1,0:T(8,128)(2,1)}, u32[]{:S(2)}) copy-start(bf16[16,4,32,128]{3,2,1,0:T(8,128)(2,1)} %get-tuple-element.14) | copy-start | bytes 1572868
  81.1 8.7 %copy-start.13 = (bf16[16,4,32,128]{3,2,1,0:T(8,128)(2,1)S(1)}, bf16[16,4,32,128]{3,2,1,0:T(8,128)(2,1)}, u32[]{:S(2)}) copy-start(bf16[16,4,32,128]{3,2,1,0:T(8,128)(2,1)} %get-tuple-element.15) | copy-start | bytes 1572868
  83.1 7.6 %copy-start.12 = (bf16[16,4,32,128]{3,2,1,0:T(8,128)(2,1)S(1)}, bf16[16,4,32,128]{3,2,1,0:T(8,128)(2,1)}, u32[]{:S(2)}) copy-start(bf16[16,4,32,128]{3,2,1,0:T(8,128)(2,1)} %get-tuple-element.16) | copy-start | bytes 1572868
  84.8 7.6 %copy-start.11 = (bf16[16,4,32,128]{3,2,1,0:T(8,128)(2,1)S(1)}, bf16[16,4,32,128]{3,2,1,0:T(8,128)(2,1)}, u32[]{:S(2)}) copy-start(bf16[16,4,32,128]{3,2,1,0:T(8,128)(2,1)} %get-tuple-element.17) | copy-start | bytes 1572868
  89.0 7.6 %copy-start.35 = (bf16[16,4,32,128]{3,2,1,0:T(8,128)(2,1)S(1)}, bf16[16,4,32,128]{3,2,1,0:T(8,128)(2,1)}, u32[]{:S(2)}) copy-start(bf16[16,4,32,128]{3,2,1,0:T(8,128)(2,1)} %get-tuple-element.23) | copy-start | bytes 1572868
  89.9 7.6 %copy-start.34 = (bf16[16,4,32,128]{3,2,1,0:T(8,128)(2,1)S(1)}, bf16[16,4,32,128]{3,2,1,0:T(8,128)(2,1)}, u32[]{:S(2)}) copy-start(bf16[16,4,32,128]{3,2,1,0:T(8,128)(2,1)} %get-tuple-element.24) | copy-start | bytes 1572868
  90.7 7.6 %copy-start.33 = (bf16[16,4,32,128]{3,2,1,0:T(8,128)(2,1)S(1)}, bf16[16,4,32,128]{3,2,1,0:T(8,128)(2,1)}, u32[]{:S(2)}) copy-start(bf16[16,4,32,128]{3,2,1,0:T(8,128)(2,1)} %get-tuple-element.25) | copy-start | bytes 1572868
  91.6 7.6 %copy-start.32 = (bf16[16,4,32,128]{3,2,1,0:T(8,128)(2,1)S(1)}, bf16[16,4,32,128]{3,2,1,0:T(8,128)(2,1)}, u32[]{:S(2)}) copy-start(bf16[16,4,32,128]{3,2,1,0:T(8,128)(2,1)} %get-tuple-element.26) | copy-start | bytes 1572868
  93.3 6.8 %copy-start.31 = (bf16[16,4,32,128]{3,2,1,0:T(8,128)(2,1)S(1)}, bf16[16,4,32,128]{3,2,1,0:T(8,128)(2,1)}, u32[]{:S(2)}) copy-start(bf16[16,4,32,128]{3,2,1,0:T(8,128)(2,1)} %get-tuple-element.27) | copy-start | bytes 1572868
  94.1 6.8 %copy-start.30 = (bf16[16,4,32,128]{3,2,1,0:T(8,128)(2,1)S(1)}, bf16[16,4,32,128]{3,2,1,0:T(8,128)(2,1)}, u32[]{:S(2)}) copy-start(bf16[16,4,32,128]{3,2,1,0:T(8,128)(2,1)} %get-tuple-element.28) | copy-start | bytes 1572868
  168.8 6.9 %copy-start.9 = (bf16[16,4,32,128]{3,2,1,0:T(8,128)(2,1)S(1)}, bf16[16,4,32,128]{3,2,1,0:T(8,128)(2,1)}, u32[]{:S(2)}) copy-start(bf16[16,4,32,128]{3,2,1,0:T(8,128)(2,1)} %get-tuple-element.38) | copy-start | bytes 1572868
  168.8 7.2 %copy-start.8 = (bf16[16,4,32,128]{3,2,1,0:T(8,128)(2,1)S(1)}, bf16[16,4,32,128]{3,2,1,0:T(8,128)(2,1)}, u32[]{:S(2)}) copy-start(bf16[16,4,32,128]{3,2,1,0:T(8,128)(2,1)} %get-tuple-element.39) | copy-start | bytes 1572868
  168.8 7.4 %copy-start.7 = (bf16[16,4,32,128]{3,2,1,0:T(8,128)(2,1)S(1)}, bf16[16,4,32,128]{3,2,1,0:T(8,128)(2,1)}, u32[]{:S(2)}) copy-start(bf16[16,4,32,128]{3,2,1,0:T(8,128)(2,1)} %get-tuple-element.40) | copy-start | bytes 1572868
  168.8 7.7 %copy-start.6 = (bf16[16,4,32,128]{3,2,1,0:T(8,128)(2,1)S(1)}, bf16[16,4,32,128]{3,2,1,0:T(8,128)(2,1)}, u32[]{:S(2)}) copy-start(bf16[16,4,32,128]{3,2,1,0:T(8,128)(2,1)} %get-tuple-element.41) | copy-start | bytes 1572868
  (17 other events, 61.6 us)
Sparse Core Ops, SparseCore 0:
  68.8 18.9 reduce-scatter.4
where the time goes:
time: 191 us; the launch traced here: 190 us
  blocking collectives  87.4 us (46%)
  matrix products  55.3 us (29%)
  local copies, waits for them, and re-layouts  21.9 us (11%)
  between operations  15 us (8%)
  starting transfers between devices  7.32 us (4%)
  other arithmetic  2.93 us (2%)
    all_gather x1, blocking collectives, shards(): out_all = pad_all(lax.all_gather(grad_out, 'space', axis=0, tiled=True))  38.5 us
    dot_general x54, matrix products, weight_terms(): lax.dot_general(source, window, (((1,), (0,)), ((), ())), preferred_eleme...  37.7 us
    all_gather x1, blocking collectives, shards(): pre_all = pad_all(lax.all_gather(grad_pre, 'space', axis=0, tiled=True))  31.5 us
    dot_general x54, matrix products, carry_back(): lax.dot_general(window, weight[:, tap[0], tap[1], tap[2], :], (((1,), (1,...  17.5 us
    unnamed x1, blocking collectives  17.4 us
    slice x8, local copies, waits for them, and re-layouts, window_at(): padded[2 - tap[0]:2 - tap[0] + planes, 2 - tap[1]:2 - tap[1] + height, 2...  16.7 us
    all_to_all x1, starting transfers between devices, shards(): both = lax.all_to_all(both, 'space', 1, 1)  7.28 us
  transfers between devices with their start and end apart: 2, of which 0 were waited for; matrix products, arithmetic and copies ran while one was open for 25% of the time, Pallas kernels for 0%

commit v1 on v0

--- a/solution.py
+++ b/solution.py
@@ -3,6 +3,7 @@
 import jax.numpy as jnp
 from jax import lax
 from jax.sharding import PartitionSpec as P
+from jax.lax import axis_index, axis_size, ppermute
 
 TAP_LIST = [
     (tap_depth, tap_row, tap_col)
@@ -10,6 +11,28 @@
     for tap_row in range(3)
     for tap_col in range(3)
 ]
+
+
+def touch_islands(message):
+    peer_axis = "space"
+    prior = axis_size(peer_axis)
+    main, z2, x_now = (prior, axis_index(peer_axis), message.shape[0])
+    current_block, current_arr = (message, 1)
+    while current_arr < main:
+        current_block = jnp.concatenate(
+            [
+                current_block,
+                ppermute(
+                    current_block,
+                    peer_axis,
+                    list(map(lambda hop_no: (hop_no, (hop_no - current_arr) % main), range(main))),
+                ),
+            ],
+            0,
+        )
+        current_arr = 2 * current_arr
+    y_new = jnp.roll(current_block, z2 * x_now, 0)
+    return y_new
 
 
 def window_at(padded, tap, planes, height, columns):
@@ -74,7 +97,7 @@
         pre_hidden, lax.axis_index("filt") * group_width, group_width, 3
     )
     grad_pre = jnp.where(own_pre > 0, grad_hidden, jnp.zeros_like(grad_hidden)).astype(jnp.bfloat16)
-    pre_all = pad_all(lax.all_gather(grad_pre, "space", axis=0, tiled=True))
+    pre_all = pad_all(touch_islands(grad_pre))
     pre_pad = lax.dynamic_slice_in_dim(pre_all, start, planes + 2, 0)
     input_partial = carry_back(pre_pad, weight_one, planes, height, columns)
     grad_rows = lax.psum_scatter(input_partial, "filt", scatter_dimension=1, tiled=True)

time: 191 us -> 178 us (0.932)
  blocking collectives: 87.4 us -> 56.2 us
  waiting for transfers between devices: 0.02 us -> 17.4 us
    all_gather x1 -> x0, blocking collectives: 31.5 us -> none  [shards(): pre_all = pad_all(lax.all_gather(grad_pre, 'space', axis=0, tiled=True))]
    ppermute x0 -> x3, waiting for transfers between devices: none -> 17.3 us  [touch_islands(): ppermute(current_block, peer_axis, list(map(lambda hop_no: (hop_no, (hop_...]
  transfers between devices with their start and end apart: 2 -> 5, of which waited for: 0 -> 3; matrix products, arithmetic and copies ran while one was open for 25% -> 27% of each run, Pallas kernels for 0% -> 0%
where the time goes in v1:
time: 178 us
  blocking collectives  56.2 us (32%)
  matrix products  55.3 us (31%)
  local copies, waits for them, and re-layouts  22.4 us (13%)
  waiting for transfers between devices  17.4 us (10%)
  between operations  15.1 us (8%)
  starting transfers between devices  8.28 us (5%)
  other arithmetic  2.98 us (2%)
    all_gather x1, blocking collectives, shards(): out_all = pad_all(lax.all_gather(grad_out, 'space', axis=0, tiled=True))  38.5 us
    dot_general x54, matrix products, weight_terms(): lax.dot_general(source, window, (((1,), (0,)), ((), ())), preferred_eleme...  37.7 us
    unnamed x1, blocking collectives  17.6 us
    dot_general x54, matrix products, carry_back(): lax.dot_general(window, weight[:, tap[0], tap[1], tap[2], :], (((1,), (1,...  17.5 us
    ppermute x3, waiting for transfers between devices, touch_islands(): ppermute(current_block, peer_axis, list(map(lambda hop_no: (hop_no, (hop_...  17.3 us
    slice x8, local copies, waits for them, and re-layouts, window_at(): padded[2 - tap[0]:2 - tap[0] + planes, 2 - tap[1]:2 - tap[1] + height, 2...  16.3 us
    all_to_all x1, starting transfers between devices, shards(): both = lax.all_to_all(both, 'space', 1, 1)  7.28 us
  transfers between devices with their start and end apart: 5, of which 3 were waited for; matrix products, arithmetic and copies ran while one was open for 27% of the time, Pallas kernels for 0%

profile of v1, /device:TPU:0, one launch (start us, length us, event | category | flops | bytes accessed | tf_op | source)
XLA Modules:
  0.0 177.6 jit_solution(17445497335372553836)
XLA Ops:
  10.2 7.3 %all-to-all-start = ((bf16[2,8,64,256]{3,2,0,1:T(8,128)(2,1)}), bf16[2,8,64,256]{3,2,0,1:T(8,128)(2,1)}, u32[]{:S(2)}, u32[]{:S(2)}) async-start(bf16[2,8,64,256]{3,2,0,1:T(8,128)(2,1)} %copy.16), calls=%async_computation.1 | async-start | bytes 1048576 | tf_op jit(solution)/shard_map/all_to_all | solution.py:91
  17.6 38.5 %all_gather.3 = bf16[16,4,32,128]{3,2,1,0:T(8,128)(2,1)S(1)} all-gather(bf16[2,4,32,128]{3,2,1,0:T(8,128)(2,1)S(1)} %copy-done.37), channel_id=1, replica_groups=mesh['space'=8,'filt'=4] {'space'}, dimensions={0}, use_global_device_ids=true | all-gather | bytes 589824 | tf_op jit(solution)/shard_map/all_gather | solution.py:86
  57.9 1.1 fusion.162
  59.0 1.1 convolution_add_fusion.51
  60.1 1.1 convolution_add_fusion.50
  61.3 1.1 convolution_add_fusion.49
  69.3 2.2 %pad_slice_fusion.27 = (bf16[16,4,32,128]{3,2,1,0:T(8,128)(2,1)}, bf16[16,4,32,128]{3,2,1,0:T(8,128)(2,1)}, bf16[16,4,32,128]{3,2,1,0:T(8,128)(2,1)}, bf16[16,4,...) fusion(bf16[16,4,32,128]{3,2,1,0:T(8,128)(2,1)S(1)} %all_gather.3), kind=kLoop, calls=%fused_computation.80 | loop fusion | bytes 4194304 | tf_op jit(solution)/shard_map/slice | solution.py:39
  71.5 4.2 %pad_slice_fusion.26 = (bf16[16,4,32,128]{3,2,1,0:T(8,128)(2,1)S(1)}, bf16[16,4,32,128]{3,2,1,0:T(8,128)(2,1)}, bf16[16,4,32,128]{3,2,1,0:T(8,128)(2,1)}, bf16[1...) fusion(bf16[16,4,32,128]{3,2,1,0:T(8,128)(2,1)S(1)} %all_gather.3), kind=kLoop, calls=%fused_computation.79 | loop fusion | bytes 10485760 | tf_op jit(solution)/shard_map/slice | solution.py:39
  75.8 1.9 %fusion.218 = (bf16[1,64,8,256]{3,1,0,2:T(8,128)(2,1)S(1)}, bf16[1,64,8,256]{3,1,0,2:T(8,128)(2,1)}) fusion(bf16[2,64,8,256]{3,1,0,2:T(8,128)(2,1)} %bitcast.114), kind=kLoop, calls=%fused_computation.445 | loop fusion | bytes 1048576 | tf_op jit(solution)/shard_map/slice | solution.py:106
  77.8 2.0 %fusion.53 = f32[64,27,128]{2,0,1:T(8,128)} fusion(bf16[64,2048]{1,0:T(8,128)(2,1)S(1)} %bitcast.700, bf16[2048,128]{1,0:T(8,128)(2,1)} %bitcast.766), kind=kOutput, calls=%fused_computation.238 | convolution fusion | flops 33562624 | bytes 819200 | tf_op jit(solution)/shard_map/dot_general | solution.py:67
  79.7 1.9 %fusion.51 = f32[64,27,128]{2,0,1:T(8,128)} fusion(f32[64,27,128]{2,0,1:T(8,128)} %fusion.53, bf16[64,2048]{1,0:T(8,128)(2,1)S(1)} %bitcast.701, bf16[2048,128]{1,0:T(8,128)(2,1)} %bitcast.765), kind=kOutput, calls=%fused_computation.235 | convolution fusion | flops 33562624 | bytes 819200 | tf_op jit(solution)/shard_map/dot_general | solution.py:67
  81.7 1.9 %fusion.49 = f32[64,27,128]{2,0,1:T(8,128)} fusion(f32[64,27,128]{2,0,1:T(8,128)} %fusion.51, bf16[64,2048]{1,0:T(8,128)(2,1)S(1)} %bitcast.702, bf16[2048,128]{1,0:T(8,128)(2,1)} %bitcast.764), kind=kOutput, calls=%fused_computation.232 | convolution fusion | flops 33562624 | bytes 819200 | tf_op jit(solution)/shard_map/dot_general | solution.py:67
  103.3 3.4 %collective-permute-done = bf16[2,4,32,128]{3,2,1,0:T(8,128)(2,1)S(1)} collective-permute-done((bf16[2,4,32,128]{3,2,1,0:T(8,128)(2,1)S(1)}, bf16[2,4,32,128]{3,2,1,0:T(8,128)(2,1)S(1)}, u32[]{:S(2)}, u32[]{:S(2)}) %collective-permute-start) | collective-permute-done | bytes 65568 | tf_op jit(solution)/shard_map/ppermute | solution.py:25
  108.4 5.8 %collective-permute-done.1 = bf16[4,4,32,128]{3,2,1,0:T(8,128)(2,1)S(1)} collective-permute-done((bf16[4,4,32,128]{3,2,1,0:T(8,128)(2,1)S(1)}, bf16[4,4,32,128]{3,2,1,0:T(8,128)(2,1)S(1)}, u32[]{:S(2)}, u32[]{:S(2)}) %collective-permute-start.1) | collective-permute-done | bytes 131104 | tf_op jit(solution)/shard_map/ppermute | solution.py:25
  115.2 8.2 %collective-permute-done.2 = bf16[8,4,32,128]{3,2,1,0:T(8,128)(2,1)S(1)} collective-permute-done((bf16[8,4,32,128]{3,2,1,0:T(8,128)(2,1)S(1)}, bf16[8,4,32,128]{3,2,1,0:T(8,128)(2,1)S(1)}, u32[]{:S(2)}, u32[]{:S(2)}) %collective-permute-start.2) | collective-permute-done | bytes 262176 | tf_op jit(solution)/shard_map/ppermute | solution.py:25
  123.5 4.3 %pad_slice_fusion = (bf16[16,4,32,128]{3,2,1,0:T(8,128)(2,1)S(1)}, bf16[16,4,32,128]{3,2,1,0:T(8,128)(2,1)}, bf16[16,4,32,128]{3,2,1,0:T(8,128)(2,1)}, bf16[16,4...) fusion(bf16[16,4,32,128]{3,2,1,0:T(8,128)(2,1)S(1)} %constant_d, ...), kind=kLoop, calls=%fused_computation.26 | loop fusion | bytes 10485760 | tf_op jit(solution)/shard_map/slice | solution.py:39
  127.8 2.2 %pad_slice_fusion.1 = (bf16[16,4,32,128]{3,2,1,0:T(8,128)(2,1)}, bf16[16,4,32,128]{3,2,1,0:T(8,128)(2,1)}, bf16[16,4,32,128]{3,2,1,0:T(8,128)(2,1)}, bf16[16,4,3...) fusion(bf16[16,4,32,128]{3,2,1,0:T(8,128)(2,1)S(1)} %constant_d, ...), kind=kLoop, calls=%fused_computation.27 | loop fusion | bytes 4194304 | tf_op jit(solution)/shard_map/slice | solution.py:39
  138.9 17.6 %all-reduce.4 = bf16[2,4,32,512]{3,2,1,0:T(8,128)(2,1)} all-reduce(f32[2,4,32,512]{3,2,1,0:T(8,128)} %bitcast.768), channel_id=3, replica_groups=mesh['space'=8,'filt'=4] {'filt'}, use_global_device_ids=true, to_apply=%region_1.2.clone | all-reduce | flops 131072 | bytes 786432
  156.6 1.4 fusion.107
  158.0 1.3 fusion.105
  159.3 1.3 fusion.103
  160.7 1.3 fusion.101
  162.0 1.3 fusion.99
  168.6 2.1 %dynamic-slice_convert_fusion = bf16[2,1,32,512]{3,2,1,0:T(8,128)(2,1)} fusion(bf16[2,4,32,512]{3,2,1,0:T(8,128)(2,1)} %all-reduce.4, u32[]{:T(128)} %bitcast.231), kind=kLoop, calls=%fused_computation.323 | loop fusion | bytes 131076 | tf_op jit(solution)/shard_map/convert_element_type | solution.py:104
  (205 shorter events, 47.8 us)
Async XLA Ops:
  7.2 10.4 %copy-start.37 = (bf16[2,4,32,128]{3,2,1,0:T(8,128)(2,1)S(1)}, bf16[2,4,32,128]{3,2,1,0:T(8,128)(2,1)}, u32[]{:S(2)}) copy-start(bf16[2,4,32,128]{3,2,1,0:T(8,128)(2,1)} %param.9) | copy-start | bytes 196612
  10.2 65.5 %all-to-all-start = ((bf16[2,8,64,256]{3,2,0,1:T(8,128)(2,1)}), bf16[2,8,64,256]{3,2,0,1:T(8,128)(2,1)}, u32[]{:S(2)}, u32[]{:S(2)}) async-start(bf16[2,8,64,256]{3,2,0,1:T(8,128)(2,1)} %copy.16), calls=%async_computation.1 | async-start | bytes 1048576 | tf_op jit(solution)/shard_map/all_to_all | solution.py:91
  17.5 83.9 %reduce-scatter.5.cloned.1.call-start = ((), (), s32[]{:S(2)}) async-start(), calls=%async_computation.2 | async-start | bytes 655360 | tf_op jit(solution)/shard_map/reduce_scatter | solution.py:94
  75.8 7.9 %copy-start.21 = (bf16[16,4,32,128]{3,2,1,0:T(8,128)(2,1)S(1)}, bf16[16,4,32,128]{3,2,1,0:T(8,128)(2,1)}, u32[]{:S(2)}) copy-start(bf16[16,4,32,128]{3,2,1,0:T(8,128)(2,1)} %get-tuple-element.9) | copy-start | bytes 1572868
  75.8 8.7 %copy-start.20 = (bf16[16,4,32,128]{3,2,1,0:T(8,128)(2,1)S(1)}, bf16[16,4,32,128]{3,2,1,0:T(8,128)(2,1)}, u32[]{:S(2)}) copy-start(bf16[16,4,32,128]{3,2,1,0:T(8,128)(2,1)} %get-tuple-element.10) | copy-start | bytes 1572868
  75.8 9.5 %copy-start.19 = (bf16[16,4,32,128]{3,2,1,0:T(8,128)(2,1)S(1)}, bf16[16,4,32,128]{3,2,1,0:T(8,128)(2,1)}, u32[]{:S(2)}) copy-start(bf16[16,4,32,128]{3,2,1,0:T(8,128)(2,1)} %get-tuple-element.11) | copy-start | bytes 1572868
  75.8 10.4 %copy-start.18 = (bf16[16,4,32,128]{3,2,1,0:T(8,128)(2,1)S(1)}, bf16[16,4,32,128]{3,2,1,0:T(8,128)(2,1)}, u32[]{:S(2)}) copy-start(bf16[16,4,32,128]{3,2,1,0:T(8,128)(2,1)} %get-tuple-element.12) | copy-start | bytes 1572868
  75.8 11.2 %copy-start.17 = (bf16[16,4,32,128]{3,2,1,0:T(8,128)(2,1)S(1)}, bf16[16,4,32,128]{3,2,1,0:T(8,128)(2,1)}, u32[]{:S(2)}) copy-start(bf16[16,4,32,128]{3,2,1,0:T(8,128)(2,1)} %get-tuple-element.13) | copy-start | bytes 1572868
  77.7 10.1 %copy-start.16 = (bf16[16,4,32,128]{3,2,1,0:T(8,128)(2,1)S(1)}, bf16[16,4,32,128]{3,2,1,0:T(8,128)(2,1)}, u32[]{:S(2)}) copy-start(bf16[16,4,32,128]{3,2,1,0:T(8,128)(2,1)} %get-tuple-element.14) | copy-start | bytes 1572868
  77.8 11.0 %copy-start.15 = (bf16[16,4,32,128]{3,2,1,0:T(8,128)(2,1)S(1)}, bf16[16,4,32,128]{3,2,1,0:T(8,128)(2,1)}, u32[]{:S(2)}) copy-start(bf16[16,4,32,128]{3,2,1,0:T(8,128)(2,1)} %get-tuple-element.15) | copy-start | bytes 1572868
  79.7 9.8 %copy-start.14 = (bf16[16,4,32,128]{3,2,1,0:T(8,128)(2,1)S(1)}, bf16[16,4,32,128]{3,2,1,0:T(8,128)(2,1)}, u32[]{:S(2)}) copy-start(bf16[16,4,32,128]{3,2,1,0:T(8,128)(2,1)} %get-tuple-element.16) | copy-start | bytes 1572868
  81.7 8.7 %copy-start.13 = (bf16[16,4,32,128]{3,2,1,0:T(8,128)(2,1)S(1)}, bf16[16,4,32,128]{3,2,1,0:T(8,128)(2,1)}, u32[]{:S(2)}) copy-start(bf16[16,4,32,128]{3,2,1,0:T(8,128)(2,1)} %get-tuple-element.17) | copy-start | bytes 1572868
  83.6 7.6 %copy-start.12 = (bf16[16,4,32,128]{3,2,1,0:T(8,128)(2,1)S(1)}, bf16[16,4,32,128]{3,2,1,0:T(8,128)(2,1)}, u32[]{:S(2)}) copy-start(bf16[16,4,32,128]{3,2,1,0:T(8,128)(2,1)} %get-tuple-element.18) | copy-start | bytes 1572868
  85.3 7.6 %copy-start.11 = (bf16[16,4,32,128]{3,2,1,0:T(8,128)(2,1)S(1)}, bf16[16,4,32,128]{3,2,1,0:T(8,128)(2,1)}, u32[]{:S(2)}) copy-start(bf16[16,4,32,128]{3,2,1,0:T(8,128)(2,1)} %get-tuple-element.19) | copy-start | bytes 1572868
  89.6 7.6 %copy-start.35 = (bf16[16,4,32,128]{3,2,1,0:T(8,128)(2,1)S(1)}, bf16[16,4,32,128]{3,2,1,0:T(8,128)(2,1)}, u32[]{:S(2)}) copy-start(bf16[16,4,32,128]{3,2,1,0:T(8,128)(2,1)} %get-tuple-element.25) | copy-start | bytes 1572868
  92.1 7.6 %copy-start.32 = (bf16[16,4,32,128]{3,2,1,0:T(8,128)(2,1)S(1)}, bf16[16,4,32,128]{3,2,1,0:T(8,128)(2,1)}, u32[]{:S(2)}) copy-start(bf16[16,4,32,128]{3,2,1,0:T(8,128)(2,1)} %get-tuple-element.28) | copy-start | bytes 1572868
  93.0 7.6 %copy-start.31 = (bf16[16,4,32,128]{3,2,1,0:T(8,128)(2,1)S(1)}, bf16[16,4,32,128]{3,2,1,0:T(8,128)(2,1)}, u32[]{:S(2)}) copy-start(bf16[16,4,32,128]{3,2,1,0:T(8,128)(2,1)} %get-tuple-element.29) | copy-start | bytes 1572868
  94.6 7.8 %copy-start.30 = (bf16[16,4,32,128]{3,2,1,0:T(8,128)(2,1)S(1)}, bf16[16,4,32,128]{3,2,1,0:T(8,128)(2,1)}, u32[]{:S(2)}) copy-start(bf16[16,4,32,128]{3,2,1,0:T(8,128)(2,1)} %get-tuple-element.30) | copy-start | bytes 1572868
  95.5 12.0 %copy-start.29 = (bf16[16,4,32,128]{3,2,1,0:T(8,128)(2,1)S(1)}, bf16[16,4,32,128]{3,2,1,0:T(8,128)(2,1)}, u32[]{:S(2)}) copy-start(bf16[16,4,32,128]{3,2,1,0:T(8,128)(2,1)} %get-tuple-element.24) | copy-start | bytes 1572868
  98.0 17.1 %copy-start.36 = (bf16[1,64,8,256]{3,1,0,2:T(8,128)(2,1)S(1)}, bf16[1,64,8,256]{3,1,0,2:T(8,128)(2,1)}, u32[]{:S(2)}) copy-start(bf16[1,64,8,256]{3,1,0,2:T(8,128)(2,1)} %get-tuple-element.32) | copy-start | bytes 786436
  102.4 4.3 %collective-permute-start = (bf16[2,4,32,128]{3,2,1,0:T(8,128)(2,1)S(1)}, bf16[2,4,32,128]{3,2,1,0:T(8,128)(2,1)S(1)}, u32[]{:S(2)}, u32[]{:S(2)}) collective-permute-start(bf16[2,4,32,128]{3,2,1,0:T(8,128)(2,1)S(1)} %get-tuple-element.4), channel_id=1, source_target_pairs={{0,28},{4,0},{8,4},{12,8},{16,12},{20,16},{24,20},{28,24},{1,29},{... | collective-permute-start | bytes 196616 | tf_op jit(solution)/shard_map/ppermute | solution.py:25
  106.7 7.4 %collective-permute-start.1 = (bf16[4,4,32,128]{3,2,1,0:T(8,128)(2,1)S(1)}, bf16[4,4,32,128]{3,2,1,0:T(8,128)(2,1)S(1)}, u32[]{:S(2)}, u32[]{:S(2)}) collective-permute-start(bf16[4,4,32,128]{3,2,1,0:T(8,128)(2,1)S(1)} %pad_maximum_fusion.1), channel_id=1, source_target_pairs={{0,24},{4,28},{8,0},{12,4},{16,8},{20,12},{24,16},{28,20},{1,25},{... | collective-permute-start | bytes 393224 | tf_op jit(solution)/shard_map/ppermute | solution.py:25
  114.2 9.2 %collective-permute-start.2 = (bf16[8,4,32,128]{3,2,1,0:T(8,128)(2,1)S(1)}, bf16[8,4,32,128]{3,2,1,0:T(8,128)(2,1)S(1)}, u32[]{:S(2)}, u32[]{:S(2)}) collective-permute-start(bf16[8,4,32,128]{3,2,1,0:T(8,128)(2,1)S(1)} %pad_maximum_fusion), channel_id=1, source_target_pairs={{0,16},{4,20},{8,24},{12,28},{16,0},{20,4},{24,8},{28,12},{1,17},{... | collective-permute-start | bytes 786440 | tf_op jit(solution)/shard_map/ppermute | solution.py:25
  156.6 7.7 %copy-start.6 = (bf16[16,4,32,128]{3,2,1,0:T(8,128)(2,1)S(1)}, bf16[16,4,32,128]{3,2,1,0:T(8,128)(2,1)}, u32[]{:S(2)}) copy-start(bf16[16,4,32,128]{3,2,1,0:T(8,128)(2,1)} %get-tuple-element.43) | copy-start | bytes 1572868
  (21 other events, 91.7 us)
Sparse Core Ops, SparseCore 0:
  68.8 18.9 reduce-scatter.4
